TPU v7x, 128 devices: a whole 4x4x4 slice. The times are simulated.
128 devices in a mesh: fsdp: 16 (over y, z), seq: 8 (over x, core).
Axes of the slice: x: 4, y: 4, z: 4, core: 2. Of those that a mesh axis runs over, the one named last changes fastest.
Arguments:
- frames: bfloat16 [16, 3072, 1536], P('fsdp', 'seq'), may hold values from -0.59765625 to 0.59765625
- lengths: int32 [16, 12], P('fsdp'), may hold values from 1 to 512, 3072 in all within a row
- w_qkv: bfloat16 [1536, 3072], P('fsdp'), may hold values from -4 to 4
- d_context: bfloat16 [16, 3072, 1024], P('fsdp', 'seq'), may hold values from -0.59765625 to 0.59765625
Outputs:
- context: bfloat16 [16, 3072, 1024], P('fsdp', 'seq')
- grad_input: bfloat16 [16, 3072, 1536], P('fsdp', 'seq')
- grad_weight: float32 [1536, 3072], P('fsdp', 'seq')
Inputs may be any that keep to these rules, and one draw needn't show every extreme that they name: The 12 lengths of a sequence sum to 3072, and the longest is exactly 512.
All inputs are finite; a program needn't handle non-finite values.
Results may differ from a plain program's by a relative error of at most 0.018.
Values may be sent and summed in bfloat16 or wider, within the bound.
A program may use at most 128 MiB of HBM per device.

v0:
```python
import jax
import jax.numpy as jnp
from jax import lax
from jax.sharding import PartitionSpec as P

HEADS = 16
HEAD_DIM = 64
MOST = 512


def segment_ids(lengths, frame_total):
    utter_ends = jnp.cumsum(lengths)
    positions = jnp.arange(frame_total, dtype=jnp.int32)
    return jnp.sum((positions[:, None] >= utter_ends[None, :]).astype(jnp.int32), axis=1)


def attend(query, keys, values, grad_out, segment):
    frame_total = query.shape[0]
    block_rows = 512
    key_span = min(block_rows + 2 * MOST, frame_total)
    block_count = frame_total // block_rows
    score_scale = HEAD_DIM ** (-0.5)

    def block_step(block_index, state_tuple):
        context, grad_query, grad_key, grad_value = state_tuple
        block_start = (block_index * block_rows).astype(jnp.int32)
        anchor = jnp.clip(block_start - MOST, 0, frame_total - key_span)
        query_block = lax.dynamic_slice_in_dim(query, block_start, block_rows, 0)
        grad_block = lax.dynamic_slice_in_dim(grad_out, block_start, block_rows, 0)
        segment_query = lax.dynamic_slice_in_dim(segment, block_start, block_rows, 0)
        key_window = lax.dynamic_slice_in_dim(keys, anchor, key_span, 0)
        value_window = lax.dynamic_slice_in_dim(values, anchor, key_span, 0)
        segment_key = lax.dynamic_slice_in_dim(segment, anchor, key_span, 0)
        scores = (
            jnp.einsum("qhd,khd->hqk", query_block, key_window, preferred_element_type=jnp.float32)
            * score_scale
        )
        same_utterance = segment_query[:, None] == segment_key[None, :]
        scores = jnp.where(same_utterance[None], scores, -jnp.inf)
        row_max = jnp.max(scores, axis=-1, keepdims=True)
        exponent = jnp.exp(scores - row_max)
        softmax_out = exponent / jnp.sum(exponent, axis=-1, keepdims=True)
        weights = softmax_out.astype(jnp.bfloat16)
        out_block = jnp.einsum(
            "hqk,khd->qhd", weights, value_window, preferred_element_type=jnp.float32
        ).astype(jnp.bfloat16)
        value_term = jnp.einsum(
            "hqk,qhd->khd", weights, grad_block, preferred_element_type=jnp.float32
        )
        dprobs = jnp.einsum(
            "qhd,khd->hqk", grad_block, value_window, preferred_element_type=jnp.float32
        )
        dscores = (
            softmax_out
            * (dprobs - jnp.sum(softmax_out * dprobs, axis=-1, keepdims=True))
            * score_scale
        )
        dscores = dscores.astype(jnp.bfloat16)
        query_term = jnp.einsum(
            "hqk,khd->qhd", dscores, key_window, preferred_element_type=jnp.float32
        ).astype(jnp.bfloat16)
        key_term = jnp.einsum(
            "hqk,qhd->khd", dscores, query_block, preferred_element_type=jnp.float32
        )
        context = lax.dynamic_update_slice_in_dim(context, out_block, block_start, 0)
        grad_query = lax.dynamic_update_slice_in_dim(grad_query, query_term, block_start, 0)
        grad_key = lax.dynamic_update_slice_in_dim(
            grad_key, lax.dynamic_slice_in_dim(grad_key, anchor, key_span, 0) + key_term, anchor, 0
        )
        grad_value = lax.dynamic_update_slice_in_dim(
            grad_value,
            lax.dynamic_slice_in_dim(grad_value, anchor, key_span, 0) + value_term,
            anchor,
            0,
        )
        return (context, grad_query, grad_key, grad_value)

    shape_one = query.shape
    initial = (
        jnp.zeros(shape_one, jnp.bfloat16),
        jnp.zeros(shape_one, jnp.bfloat16),
        jnp.zeros(shape_one, jnp.float32),
        jnp.zeros(shape_one, jnp.float32),
    )
    context, grad_query, grad_key, grad_value = lax.fori_loop(0, block_count, block_step, initial)
    return (context, grad_query, grad_key.astype(jnp.bfloat16), grad_value.astype(jnp.bfloat16))


def per_device(frames, lengths, w_qkv, d_context):
    values_in = frames[0].astype(jnp.float32)
    frame_count = values_in.shape[0]
    rank_count = lax.axis_size("seq")
    frame_total = frame_count * rank_count
    width = HEADS * HEAD_DIM
    per_rank = width // rank_count
    heads_here = per_rank // HEAD_DIM
    average = jnp.mean(values_in, axis=1, keepdims=True)
    centred = values_in - average
    variance = jnp.mean(centred * centred, axis=1, keepdims=True)
    inverse_scale = lax.rsqrt(variance + 1e-05)
    whitened = centred * inverse_scale
    normed = whitened.astype(jnp.bfloat16)
    weight_full = lax.all_gather(w_qkv, "fsdp", axis=0, tiled=True)
    projected = jnp.dot(normed, weight_full, preferred_element_type=jnp.float32)
    qkv_frames = projected.astype(jnp.bfloat16).reshape(frame_count, 3, rank_count, per_rank)
    cotangent = d_context[0].reshape(frame_count, 1, rank_count, per_rank)
    heads_qkv, heads_cotangent = (
        lax.all_to_all(qkv_frames, "seq", split_axis=2, concat_axis=0, tiled=True),
        lax.all_to_all(cotangent, "seq", split_axis=2, concat_axis=0, tiled=True),
    )
    query = heads_qkv[:, 0, 0].reshape(frame_total, heads_here, HEAD_DIM)
    keys = heads_qkv[:, 1, 0].reshape(frame_total, heads_here, HEAD_DIM)
    values = heads_qkv[:, 2, 0].reshape(frame_total, heads_here, HEAD_DIM)
    grad_out = heads_cotangent[:, 0, 0].reshape(frame_total, heads_here, HEAD_DIM)
    segment = segment_ids(lengths[0], frame_total)
    context, grad_query, grad_key, grad_value = attend(query, keys, values, grad_out, segment)
    context_heads = context.reshape(frame_total, 1, 1, per_rank)
    grad_heads = jnp.stack([grad_query, grad_key, grad_value], axis=1).reshape(
        frame_total, 3, 1, per_rank
    )
    context_back, grad_back = (
        lax.all_to_all(context_heads, "seq", split_axis=0, concat_axis=2, tiled=True),
        lax.all_to_all(grad_heads, "seq", split_axis=0, concat_axis=2, tiled=True),
    )
    context_out = context_back.reshape(1, frame_count, width)
    grad_qkv = grad_back.reshape(frame_count, 3 * width)
    grad_normed = lax.dot_general(
        grad_qkv, weight_full, (((1,), (1,)), ((), ())), preferred_element_type=jnp.float32
    )
    grad_input = inverse_scale * (
        grad_normed
        - jnp.mean(grad_normed, axis=1, keepdims=True)
        - whitened * jnp.mean(grad_normed * whitened, axis=1, keepdims=True)
    )
    grad_input = grad_input.astype(jnp.bfloat16)[None]
    owned_rows = lax.psum_scatter(
        lax.dot_general(
            normed, grad_qkv, (((0,), (0,)), ((), ())), preferred_element_type=jnp.float32
        ).astype(jnp.bfloat16),
        "fsdp",
        scatter_dimension=0,
        tiled=True,
    )
    grad_weight = lax.psum_scatter(owned_rows, "seq", scatter_dimension=1, tiled=True).astype(
        jnp.float32
    )
    return (context_out, grad_input, grad_weight)


def solution(mesh):
    return jax.shard_map(
        per_device,
        mesh=mesh,
        in_specs=(P("fsdp", "seq", None), P("fsdp", None), P("fsdp", None), P("fsdp", "seq", None)),
        out_specs=(P("fsdp", "seq", None), P("fsdp", "seq", None), P("fsdp", "seq")),
        check_vma=False,
    )
```

profile of v0, /device:TPU:1, one launch (start us, length us, event | category | flops | bytes accessed | tf_op | source)
XLA Modules:
  0.0 690.4 jit_solution(15582703184175243166)
XLA Ops:
  10.2 5.8 all-to-all-start.1
  16.7 72.2 %all-gather.2.cloned.1.call-done = bf16[1536,3072]{1,0:T(8,128)(2,1)} async-done(((bf16[96,3072]{1,0:T(8,128)(2,1)}), bf16[1536,3072]{1,0:T(8,128)(2,1)}) %all-gather.2.cloned.1.call-update) | async-done | bytes 9437200 | tf_op jit(solution)/shard_map/all_gather | solution.py:103
  88.9 7.9 %fusion.104 = bf16[48,8,24,128]{3,1,2,0:T(8,128)(2,1)S(1)} fusion(bf16[1536,3072]{1,0:T(8,128)(2,1)} %all-gather.2.cloned.1.call-done, bf16[1,384,1536]{2,1,0:T(8,128)(2,1)S(1)} %copy-done, f32[384]{0:T(512)S(1)} %add_rsqrt_fusion, f32[384]{0:T(512)S(1)} %broadcast_multiply_fusion.2), kind=kOutput, calls=%fused_computation.73 | convolution fusion | flops 3627417600 | bytes 12979200 | tf_op jit(solution)/shard_map/dot_general | solution.py:104
  108.5 25.1 %all-to-all-done = bf16[384,3,8,128]{3,0,1,2:T(8,128)(2,1)S(1)} async-done(((bf16[384,3,8,128]{3,0,1,2:T(8,128)(2,1)}), bf16[384,3,8,128]{3,0,1,2:T(8,128)(2,1)S(1)}, u32[]{:S(2)}, u32[]{:S(2)}) %all-to-all-start) | async-done | bytes 2359328 | tf_op jit(solution)/shard_map/all_to_all | solution.py:108
  140.3 362.4 %while.21 = (s32[]{:T(128)}, bf16[3072,2,64]{0,2,1:T(8,128)(2,1)S(1)}, bf16[3072,2,64]{0,2,1:T(8,128)(2,1)}, f32[3072,2,64]{0,2,1:T(8,128)}, f32[3072,2,64]{0,2,...) while((s32[]{:T(128)}, ...), condition=%wide.region_8.9_spmd, body=%wide.region_4.8_spmd.sunk | while | flops 1655975424 | bytes 78963000 | solution.py:85
  141.0 6.2 fusion.162
  155.9 14.9 %fusion.165 = bf16[3072,2,64]{0,2,1:T(8,128)(2,1)} fusion(bf16[3072,2,64]{0,2,1:T(8,128)(2,1)} %get-tuple-element.393, s32[]{:T(128)S(6)} %select_n.55, f32[2,512,1536]{2,1,0:T(8,128)} %fusion.164, bf16[3072,2,64]{0,2,1:T(8,128)(2,1)S(1)} %copy-done.5, s32[]{:T(128)S(6)} %min.12, f32[2,512,1536]{2,1,0:T(8,128)} %get-tuple-element.374, ...), kind=kOutput, calls=%fused_computation.27.clone.1 | convolution fusion | flops 212404736 | bytes 25698312 | tf_op jit(solution)/shard_map/while/body/eval_jaxpr/hqk,khd->qhd/dot_general | solution.py:59
  170.7 14.9 %fusion.166 = f32[1536,2,64]{0,2,1:T(8,128)S(1)} fusion(f32[2,512,1536]{2,1,0:T(8,128)} %fusion.164, f32[3072,2,64]{0,2,1:T(8,128)} %get-tuple-element.394, s32[]{:T(128)S(6)} %min.12, bf16[3072,2,64]{0,2,1:T(8,128)(2,1)} %get-tuple-element.414, s32[]{:T(128)S(6)} %select_n.55, f32[2,512,1536]{2,1,0:T(8,128)} %get-tuple-element.374, ...), kind=kOutput, calls=%fused_computation.17.clone.1 | convolution fusion | flops 212535808 | bytes 26877960 | tf_op jit(solution)/shard_map/while/body/eval_jaxpr/hqk,qhd->khd/dot_general | solution.py:62
  195.7 5.5 dynamic_update_slice.49
  201.9 6.2 fusion.162
  216.8 14.9 %fusion.165 = bf16[3072,2,64]{0,2,1:T(8,128)(2,1)} fusion(bf16[3072,2,64]{0,2,1:T(8,128)(2,1)} %get-tuple-element.393, s32[]{:T(128)S(6)} %select_n.55, f32[2,512,1536]{2,1,0:T(8,128)} %fusion.164, bf16[3072,2,64]{0,2,1:T(8,128)(2,1)S(1)} %copy-done.5, s32[]{:T(128)S(6)} %min.12, f32[2,512,1536]{2,1,0:T(8,128)} %get-tuple-element.374, ...), kind=kOutput, calls=%fused_computation.27.clone.1 | convolution fusion | flops 212404736 | bytes 25698312 | tf_op jit(solution)/shard_map/while/body/eval_jaxpr/hqk,khd->qhd/dot_general | solution.py:59
  231.6 15.0 %fusion.166 = f32[1536,2,64]{0,2,1:T(8,128)S(1)} fusion(f32[2,512,1536]{2,1,0:T(8,128)} %fusion.164, f32[3072,2,64]{0,2,1:T(8,128)} %get-tuple-element.394, s32[]{:T(128)S(6)} %min.12, bf16[3072,2,64]{0,2,1:T(8,128)(2,1)} %get-tuple-element.414, s32[]{:T(128)S(6)} %select_n.55, f32[2,512,1536]{2,1,0:T(8,128)} %get-tuple-element.374, ...), kind=kOutput, calls=%fused_computation.17.clone.1 | convolution fusion | flops 212535808 | bytes 26877960 | tf_op jit(solution)/shard_map/while/body/eval_jaxpr/hqk,qhd->khd/dot_general | solution.py:62
  246.6 5.5 dynamic_update_slice.48
  256.7 5.5 dynamic_update_slice.49
  262.8 6.2 fusion.162
  277.7 14.9 %fusion.165 = bf16[3072,2,64]{0,2,1:T(8,128)(2,1)} fusion(bf16[3072,2,64]{0,2,1:T(8,128)(2,1)} %get-tuple-element.393, s32[]{:T(128)S(6)} %select_n.55, f32[2,512,1536]{2,1,0:T(8,128)} %fusion.164, bf16[3072,2,64]{0,2,1:T(8,128)(2,1)S(1)} %copy-done.5, s32[]{:T(128)S(6)} %min.12, f32[2,512,1536]{2,1,0:T(8,128)} %get-tuple-element.374, ...), kind=kOutput, calls=%fused_computation.27.clone.1 | convolution fusion | flops 212404736 | bytes 25698312 | tf_op jit(solution)/shard_map/while/body/eval_jaxpr/hqk,khd->qhd/dot_general | solution.py:59
  292.6 14.9 %fusion.166 = f32[1536,2,64]{0,2,1:T(8,128)S(1)} fusion(f32[2,512,1536]{2,1,0:T(8,128)} %fusion.164, f32[3072,2,64]{0,2,1:T(8,128)} %get-tuple-element.394, s32[]{:T(128)S(6)} %min.12, bf16[3072,2,64]{0,2,1:T(8,128)(2,1)} %get-tuple-element.414, s32[]{:T(128)S(6)} %select_n.55, f32[2,512,1536]{2,1,0:T(8,128)} %get-tuple-element.374, ...), kind=kOutput, calls=%fused_computation.17.clone.1 | convolution fusion | flops 212535808 | bytes 26877960 | tf_op jit(solution)/shard_map/while/body/eval_jaxpr/hqk,qhd->khd/dot_general | solution.py:62
  323.6 6.2 fusion.162
  338.4 14.9 %fusion.165 = bf16[3072,2,64]{0,2,1:T(8,128)(2,1)} fusion(bf16[3072,2,64]{0,2,1:T(8,128)(2,1)} %get-tuple-element.393, s32[]{:T(128)S(6)} %select_n.55, f32[2,512,1536]{2,1,0:T(8,128)} %fusion.164, bf16[3072,2,64]{0,2,1:T(8,128)(2,1)S(1)} %copy-done.5, s32[]{:T(128)S(6)} %min.12, f32[2,512,1536]{2,1,0:T(8,128)} %get-tuple-element.374, ...), kind=kOutput, calls=%fused_computation.27.clone.1 | convolution fusion | flops 212404736 | bytes 25698312 | tf_op jit(solution)/shard_map/while/body/eval_jaxpr/hqk,khd->qhd/dot_general | solution.py:59
  353.3 15.0 %fusion.166 = f32[1536,2,64]{0,2,1:T(8,128)S(1)} fusion(f32[2,512,1536]{2,1,0:T(8,128)} %fusion.164, f32[3072,2,64]{0,2,1:T(8,128)} %get-tuple-element.394, s32[]{:T(128)S(6)} %min.12, bf16[3072,2,64]{0,2,1:T(8,128)(2,1)} %get-tuple-element.414, s32[]{:T(128)S(6)} %select_n.55, f32[2,512,1536]{2,1,0:T(8,128)} %get-tuple-element.374, ...), kind=kOutput, calls=%fused_computation.17.clone.1 | convolution fusion | flops 212535808 | bytes 26877960 | tf_op jit(solution)/shard_map/while/body/eval_jaxpr/hqk,qhd->khd/dot_general | solution.py:62
  384.2 6.2 fusion.162
  399.0 14.9 %fusion.165 = bf16[3072,2,64]{0,2,1:T(8,128)(2,1)} fusion(bf16[3072,2,64]{0,2,1:T(8,128)(2,1)} %get-tuple-element.393, s32[]{:T(128)S(6)} %select_n.55, f32[2,512,1536]{2,1,0:T(8,128)} %fusion.164, bf16[3072,2,64]{0,2,1:T(8,128)(2,1)S(1)} %copy-done.5, s32[]{:T(128)S(6)} %min.12, f32[2,512,1536]{2,1,0:T(8,128)} %get-tuple-element.374, ...), kind=kOutput, calls=%fused_computation.27.clone.1 | convolution fusion | flops 212404736 | bytes 25698312 | tf_op jit(solution)/shard_map/while/body/eval_jaxpr/hqk,khd->qhd/dot_general | solution.py:59
  413.9 14.9 %fusion.166 = f32[1536,2,64]{0,2,1:T(8,128)S(1)} fusion(f32[2,512,1536]{2,1,0:T(8,128)} %fusion.164, f32[3072,2,64]{0,2,1:T(8,128)} %get-tuple-element.394, s32[]{:T(128)S(6)} %min.12, bf16[3072,2,64]{0,2,1:T(8,128)(2,1)} %get-tuple-element.414, s32[]{:T(128)S(6)} %select_n.55, f32[2,512,1536]{2,1,0:T(8,128)} %get-tuple-element.374, ...), kind=kOutput, calls=%fused_computation.17.clone.1 | convolution fusion | flops 212535808 | bytes 26877960 | tf_op jit(solution)/shard_map/while/body/eval_jaxpr/hqk,qhd->khd/dot_general | solution.py:62
  443.8 6.2 fusion.162
  458.6 14.9 %fusion.165 = bf16[3072,2,64]{0,2,1:T(8,128)(2,1)} fusion(bf16[3072,2,64]{0,2,1:T(8,128)(2,1)} %get-tuple-element.393, s32[]{:T(128)S(6)} %select_n.55, f32[2,512,1536]{2,1,0:T(8,128)} %fusion.164, bf16[3072,2,64]{0,2,1:T(8,128)(2,1)S(1)} %copy-done.5, s32[]{:T(128)S(6)} %min.12, f32[2,512,1536]{2,1,0:T(8,128)} %get-tuple-element.374, ...), kind=kOutput, calls=%fused_computation.27.clone.1 | convolution fusion | flops 212404736 | bytes 25698312 | tf_op jit(solution)/shard_map/while/body/eval_jaxpr/hqk,khd->qhd/dot_general | solution.py:59
  473.5 15.0 %fusion.166 = f32[1536,2,64]{0,2,1:T(8,128)S(1)} fusion(f32[2,512,1536]{2,1,0:T(8,128)} %fusion.164, f32[3072,2,64]{0,2,1:T(8,128)} %get-tuple-element.394, s32[]{:T(128)S(6)} %min.12, bf16[3072,2,64]{0,2,1:T(8,128)(2,1)} %get-tuple-element.414, s32[]{:T(128)S(6)} %select_n.55, f32[2,512,1536]{2,1,0:T(8,128)} %get-tuple-element.374, ...), kind=kOutput, calls=%fused_computation.17.clone.1 | convolution fusion | flops 212535808 | bytes 26877960 | tf_op jit(solution)/shard_map/while/body/eval_jaxpr/hqk,qhd->khd/dot_general | solution.py:62
  512.2 40.8 %all_to_all.63 = bf16[3072,3,1,128]{3,1,2,0:T(4,128)(2,1)S(1)} all-to-all(bf16[3072,3,1,128]{3,1,2,0:T(4,128)(2,1)S(1)} %copy.83), channel_id=1, replica_groups=mesh['fsdp'=16,'seq'=8] {'seq'}, dimensions={0} | all-to-all | bytes 4718592 | tf_op jit(solution)/shard_map/all_to_all | solution.py:123
  555.9 9.5 %convolution_convert_fusion = bf16[1536,3072]{1,0:T(8,128)(2,1)} fusion(bf16[384,3072]{0,1:T(8,128)(2,1)} %bitcast.107, bf16[1,384,1536]{2,1,0:T(8,128)(2,1)S(1)} %copy-done.1, f32[384]{0:T(512)S(1)} %copy-done.9, f32[384]{0:T(512)S(1)} %copy-done.7), kind=kOutput, calls=%fused_computation.54 | convolution fusion | flops 3630956544 | bytes 12979200 | tf_op jit(solution)/shard_map/dot_general | solution.py:137
  568.3 15.6 %all_to_all.64 = bf16[8,2,24576]{2,1,0:T(2,128)(2,1)S(1)} all-to-all(bf16[8,2,24576]{2,1,0:T(2,128)(2,1)S(1)} %reshape.126), channel_id=1, replica_groups=mesh['fsdp'=16,'seq'=8] {'seq'}, dimensions={0} | all-to-all | bytes 1572864 | tf_op jit(solution)/shard_map/all_to_all | solution.py:122
  586.3 63.7 %reduce-scatter.5.cloned.1.call-done = bf16[96,3072]{1,0:T(8,128)(2,1)} async-done(((bf16[1536,3072]{1,0:T(8,128)(2,1)}), bf16[96,3072]{1,0:T(8,128)(2,1)}) %reduce-scatter.5.cloned.1.call-update) | async-done | bytes 589840 | tf_op jit(solution)/shard_map/reduce_scatter | solution.py:136
  652.3 7.7 %fusion.113 = (f32[384]{0:T(512)S(1)}, f32[384]{0:T(512)S(1)}, f32[384,1536]{1,0:T(8,128)S(1)}) fusion(f32[384]{0:T(512)S(1)} %copy-done.9, f32[384]{0:T(512)S(1)} %copy-done.7, bf16[1,384,1536]{2,1,0:T(8,128)(2,1)S(1)} %copy-done.1, bf16[384,3072]{0,1:T(8,128)(2,1)} %bitcast.108, bf16[1536,3072]{1,0:T(8,128)(2,1)} %all-gather.2.cloned.1.call-done), kind=kOutput, calls=%fused_computation.86 | convolution fusion | flops 3627416576 | bytes 15341568 | tf_op jit(solution)/shard_map/dot_general | solution.py:127
  661.7 20.5 %reduce-scatter.7.cloned.1.call-done = bf16[384,96]{1,0:T(8,128)(2,1)} async-done(((bf16[3072,96]{1,0:T(8,128)(2,1)}), bf16[384,96]{1,0:T(8,128)(2,1)}) %reduce-scatter.7.cloned.1.call-update) | async-done | bytes 73744
  (124 shorter events, 174.8 us)
Async XLA Ops:
  7.2 8.8 %copy-start = (bf16[1,384,1536]{2,1,0:T(8,128)(2,1)S(1)}, bf16[1,384,1536]{2,1,0:T(8,128)(2,1)}, u32[]{:S(2)}) copy-start(bf16[1,384,1536]{2,1,0:T(8,128)(2,1)} %param.6) | copy-start | bytes 3538948
  7.2 81.8 %all-gather.2.cloned.1.call-start = ((), (), s32[]{:S(2)}) async-start(), calls=%async_computation.6 | async-start | bytes 10027008 | tf_op jit(solution)/shard_map/all_gather | solution.py:103
  10.2 89.2 %all-to-all-start.1 = ((bf16[384,1,8,128]{0,3,1,2:T(8,128)(2,1)}), bf16[384,1,8,128]{0,3,1,2:T(8,128)(2,1)S(1)}, u32[]{:S(2)}, u32[]{:S(2)}) async-start(bf16[384,1,8,128]{0,3,1,2:T(8,128)(2,1)} %bitcast.15), calls=%async_computation.1 | async-start | bytes 1572864 | tf_op jit(solution)/shard_map/all_to_all | solution.py:109
  16.2 80.6 %copy-start.6 = (f32[384]{0:T(512)}, f32[384]{0:T(512)S(1)}, u32[]{:S(2)}) copy-start(f32[384]{0:T(512)S(1)} %broadcast_multiply_fusion.2) | copy-start | bytes 4612
  16.7 80.2 %copy-start.8 = (f32[384]{0:T(512)}, f32[384]{0:T(512)S(1)}, u32[]{:S(2)}) copy-start(f32[384]{0:T(512)S(1)} %add_rsqrt_fusion) | copy-start | bytes 4612
  99.4 5.2 copy-start.10
  99.4 34.2 %all-to-all-start = ((bf16[384,3,8,128]{3,0,1,2:T(8,128)(2,1)}), bf16[384,3,8,128]{3,0,1,2:T(8,128)(2,1)S(1)}, u32[]{:S(2)}, u32[]{:S(2)}) async-start(bf16[384,3,8,128]{3,0,1,2:T(8,128)(2,1)} %copy.74), calls=%async_computation | async-start | bytes 4718592 | tf_op jit(solution)/shard_map/all_to_all | solution.py:108
  104.6 545.5 %reduce-scatter.5.cloned.1.call-start = ((), (), s32[]{:S(2)}) async-start(), calls=%async_computation.7 | async-start | bytes 10027008 | tf_op jit(solution)/shard_map/reduce_scatter | solution.py:136
  141.0 6.2 copy-start.5
  201.9 6.2 copy-start.5
  262.8 6.2 copy-start.5
  323.6 6.2 copy-start.5
  384.2 6.2 copy-start.5
  443.8 6.2 copy-start.5
  502.8 2.3 copy-start.3
  502.8 2.2 copy-start.2
  553.4 2.5 copy-start.1
  553.4 2.5 copy-start.7
  553.4 2.5 copy-start.9
  565.4 1.1 copy-start.4
  565.4 116.7 %reduce-scatter.7.cloned.1.call-start = ((), (), s32[]{:S(2)}) async-start(), calls=%async_computation.8 | async-start | bytes 884736
Sparse Core Ops, SparseCore 0:
  10.2 78.7 all-gather.1
  565.6 84.4 reduce-scatter.4
  652.5 29.6 reduce-scatter.6
where the time goes:
time: 695 us; the launch traced here: 690 us
  matrix products  320 us (46%)
  waiting for transfers between devices  182 us (26%)
  local copies, waits for them, and re-layouts  93.8 us (13%)
  blocking collectives  56.4 us (8%)
  between operations  14 us (2%)
  other arithmetic  12.3 us (2%)
  starting transfers between devices  11.1 us (2%)
    dot_general x6, matrix products, block_step(): jnp.einsum('hqk,qhd->khd', dscores, query_block, preferred_element_type=j...  89.7 us
    dot_general x6, matrix products, block_step(): jnp.einsum('hqk,khd->qhd', dscores, key_window, preferred_element_type=jn...  89.2 us
    all_gather x1, waiting for transfers between devices, per_device(): weight_full = lax.all_gather(w_qkv, 'fsdp', axis=0, tiled=True)  72.2 us
    reduce_scatter x1, waiting for transfers between devices, per_device(): lax.psum_scatter(lax.dot_general(normed, grad_qkv, (((0,), (0,)), ((), ()...  63.7 us
    all_to_all x1, blocking collectives, per_device(): lax.all_to_all(grad_heads, 'seq', split_axis=0, concat_axis=2, tiled=True)  40.8 us
    sub x6, matrix products, block_step(): exponent = jnp.exp(scores - row_max)  37.2 us
    dynamic_update_slice x6, local copies, waits for them, and re-layouts, block_step(): lax.dynamic_update_slice_in_dim(grad_value, lax.dynamic_slice_in_dim(grad...  31.5 us
    dynamic_update_slice x6, local copies, waits for them, and re-layouts, block_step(): lax.dynamic_update_slice_in_dim(grad_key, lax.dynamic_slice_in_dim(grad_k...  31.5 us
  transfers between devices with their start and end apart: 5, of which 4 were waited for; matrix products, arithmetic and copies ran while one was open for 5% of the time, Pallas kernels for 0%

commit v1 on v0

v1 whole, which is shorter than its diff:
```python
import functools

import jax
import jax.numpy as jnp
from jax import lax
from jax.experimental import pallas as pl
from jax.experimental.pallas import tpu as pltpu
from jax.sharding import PartitionSpec as P

LOG2E = 1.4426950408889634
NT = (((1,), (1,)), ((), ()))
TN = (((0,), (0,)), ((), ()))


def attend_body(total, unroll, len_ref, qkv_ref, do_ref, ctx_ref, grad_ref, gk_t, gv_t):
    lane = lax.broadcasted_iota(jnp.int32, (128, 128), 1)
    low = lane < 64

    def twice(x):
        zero = jnp.zeros_like(x)
        return jnp.concatenate([jnp.where(low, x, zero), jnp.where(low, zero, x)], axis=0)

    def fold(x):
        return jnp.where(low, x[:128], x[128:])

    def window(span, start, end):
        base = pl.multiple_of(jnp.minimum((start // 16) * 16, total - span), 16)
        key_pos = base + lax.broadcasted_iota(jnp.int32, (1, span), 1)
        bias = jnp.where((key_pos >= start) & (key_pos < end), 0.0, -1e30).astype(jnp.float32)
        gk_t[:, :span] = jnp.zeros((128, span), jnp.float32)
        gv_t[:, :span] = jnp.zeros((128, span), jnp.float32)

        def block(index, _):
            row = pl.multiple_of(base + index * 128, 16)
            rows = pl.ds(row, 128)
            keys = qkv_ref[pl.ds(base, span), 128:256]
            values = qkv_ref[pl.ds(base, span), 256:384]
            row_pos = row + lax.broadcasted_iota(jnp.int32, (128, 128), 0)
            valid = (row_pos >= start) & (row_pos < end)
            query = twice(qkv_ref[rows, 0:128])
            cot = jnp.where(valid, do_ref[rows, :].astype(jnp.float32), 0.0)
            cot = twice(cot)
            s = lax.dot_general(query, keys, NT, preferred_element_type=jnp.float32)
            s = s * (0.125 * LOG2E) + bias
            e = jnp.exp2(s - jnp.max(s, axis=1, keepdims=True))
            inv = 1.0 / jnp.sum(e, axis=1, keepdims=True)
            weights = e.astype(jnp.bfloat16)
            ctx = jnp.dot(weights, values, preferred_element_type=jnp.float32) * inv
            cot_n = cot * inv
            delta = jnp.sum(cot_n * ctx, axis=1, keepdims=True)
            cot_b = cot_n.astype(jnp.bfloat16)
            dp = lax.dot_general(cot_b, values, NT, preferred_element_type=jnp.float32)
            ds = (e * (dp - delta)).astype(jnp.bfloat16)
            gv_t[:, :span] += lax.dot_general(cot_b, weights, TN, preferred_element_type=jnp.float32)
            gk_t[:, :span] += lax.dot_general(query, ds, TN, preferred_element_type=jnp.float32)
            gq = jnp.dot(ds, keys, preferred_element_type=jnp.float32)
            ctx_ref[rows, :] = jnp.where(valid, fold(ctx), ctx_ref[rows, :].astype(jnp.float32)).astype(jnp.bfloat16)
            grad_ref[rows, 0:128] = jnp.where(
                valid, fold(gq) * 0.125, grad_ref[rows, 0:128].astype(jnp.float32)).astype(jnp.bfloat16)
            return 0

        lax.fori_loop(0, span // 128, block, 0, unroll=min(unroll, span // 128) if unroll else True)
        for part in range(span // 128):
            rows = pl.ds(pl.multiple_of(base + part * 128, 16), 128)
            row_pos = base + part * 128 + lax.broadcasted_iota(jnp.int32, (128, 128), 0)
            valid = (row_pos >= start) & (row_pos < end)
            cols = slice(part * 128, part * 128 + 128)
            gk = gk_t[:, cols].T * 0.125
            gv = gv_t[:, cols].T
            grad_ref[rows, 128:256] = jnp.where(
                valid, gk, grad_ref[rows, 128:256].astype(jnp.float32)).astype(jnp.bfloat16)
            grad_ref[rows, 256:384] = jnp.where(
                valid, gv, grad_ref[rows, 256:384].astype(jnp.float32)).astype(jnp.bfloat16)

    def utterance(index, start):
        end = start + len_ref[index]
        tiles = (end - (start // 16) * 16 + 127) // 128
        for count in range(1, 6):
            @pl.when(tiles == count)
            def _():
                window(count * 128, start, end)
        return end

    lax.fori_loop(0, len_ref.shape[0], utterance, jnp.int32(0))


def attend(lengths, qkv, cot, unroll=1):
    total = qkv.shape[0]
    return pl.pallas_call(
        functools.partial(attend_body, total, unroll),
        out_shape=(jax.ShapeDtypeStruct((total, 128), jnp.bfloat16),
                   jax.ShapeDtypeStruct((total, 384), jnp.bfloat16)),
        in_specs=[pl.BlockSpec(memory_space=pltpu.SMEM)] + [pl.BlockSpec(memory_space=pltpu.VMEM)] * 2,
        out_specs=(pl.BlockSpec(memory_space=pltpu.VMEM),) * 2,
        scratch_shapes=[pltpu.VMEM((128, 640), jnp.float32)] * 2,
        name="attention",
    )(lengths, qkv, cot)


def per_device(frames, lengths, w_qkv, d_context):
    values_in = frames[0].astype(jnp.float32)
    frame_count, model = values_in.shape
    ranks = lax.axis_size("seq")
    rank = lax.axis_index("seq")
    total = frame_count * ranks
    width = d_context.shape[2]
    per_rank = width // ranks
    average = jnp.mean(values_in, axis=1, keepdims=True)
    centred = values_in - average
    variance = jnp.mean(centred * centred, axis=1, keepdims=True)
    inverse_scale = lax.rsqrt(variance + 1e-05)
    whitened = centred * inverse_scale
    normed = whitened.astype(jnp.bfloat16)
    rows = w_qkv.shape[0]
    own = lax.dynamic_slice_in_dim(w_qkv.reshape(rows, 3, width), rank * per_rank, per_rank, 2)
    own_full = lax.all_gather(own.reshape(rows, 3 * per_rank), "fsdp", axis=0, tiled=True)
    cot = lax.all_to_all(
        d_context[0].reshape(frame_count, ranks, per_rank).transpose(1, 0, 2), "seq", 0, 0, tiled=True
    ).reshape(total, per_rank)
    normed_full = lax.all_gather(normed, "seq", axis=0, tiled=True)
    weight_full = lax.all_gather(w_qkv, "fsdp", axis=0, tiled=True)
    qkv = jnp.dot(normed_full, own_full, preferred_element_type=jnp.float32).astype(jnp.bfloat16)
    context, grads = attend(lengths[0], qkv, cot, 5)
    context_back = lax.all_to_all(context.reshape(ranks, frame_count, per_rank), "seq", 0, 0, tiled=True)
    grads_back = lax.all_to_all(grads.reshape(ranks, frame_count, 3 * per_rank), "seq", 0, 0, tiled=True)
    partial = lax.dot_general(
        normed_full, grads, (((0,), (0,)), ((), ())), preferred_element_type=jnp.float32
    ).astype(jnp.bfloat16)
    owned = lax.psum_scatter(partial, "fsdp", scatter_dimension=0, tiled=True)
    blocks = lax.all_gather(owned.reshape(rows, 3, per_rank), "seq", axis=2, tiled=True)
    grad_weight = lax.dynamic_slice_in_dim(
        blocks.reshape(rows, 3 * width), rank * 3 * per_rank, 3 * per_rank, 1
    ).astype(jnp.float32)
    context_out = context_back.transpose(1, 0, 2).reshape(1, frame_count, width)
    grad_qkv = (
        grads_back.reshape(ranks, frame_count, 3, per_rank).transpose(1, 2, 0, 3).reshape(frame_count, 3 * width)
    )
    grad_normed = lax.dot_general(
        grad_qkv, weight_full, (((1,), (1,)), ((), ())), preferred_element_type=jnp.float32
    )
    grad_input = inverse_scale * (
        grad_normed
        - jnp.mean(grad_normed, axis=1, keepdims=True)
        - whitened * jnp.mean(grad_normed * whitened, axis=1, keepdims=True)
    )
    return context_out, grad_input.astype(jnp.bfloat16)[None], grad_weight


def solution(mesh):
    return jax.shard_map(
        per_device,
        mesh=mesh,
        in_specs=(P("fsdp", "seq", None), P("fsdp", None), P("fsdp", None), P("fsdp", "seq", None)),
        out_specs=(P("fsdp", "seq", None), P("fsdp", "seq", None), P("fsdp", "seq")),
        check_vma=False,
    )
```

time: 695 us -> 290 us (0.42)
  matrix products: 320 us -> 26 us
  local copies, waits for them, and re-layouts: 93.8 us -> 17.4 us
  blocking collectives: 56.4 us -> 14.9 us
  Pallas kernels: 0 us -> 27.8 us
  waiting for transfers between devices: 182 us -> 171 us
  other arithmetic: 12.3 us -> 4.43 us
    dot_general x32 -> x2, matrix products: 276 us -> 18.3 us  [the longest x1 9.34 us: per_device(): lax.dot_general(normed_full, grads, (((0,), (0,)), ((), ())), preferred_e...]
    all_gather x0 -> x2, waiting for transfers between devices: none -> 93.1 us  [the longest x1 57.6 us: per_device(): normed_full = lax.all_gather(normed, 'seq', axis=0, tiled=True)]
    all_gather x1, waiting for transfers between devices: 72.2 us -> 0.01 us  [per_device(): weight_full = lax.all_gather(w_qkv, 'fsdp', axis=0, tiled=True)]
    dynamic_update_slice x12 -> x0, local copies, waits for them, and re-layouts: 63 us -> none  [the longest x6 31.5 us: block_step(): lax.dynamic_update_slice_in_dim(grad_value, lax.dynamic_slice_in_dim(grad...]
    all_to_all x2 -> x0, blocking collectives: 56.4 us -> none  [the longest x1 40.8 us: per_device(): lax.all_to_all(grad_heads, 'seq', split_axis=0, concat_axis=2, tiled=True)]
    sub x6 -> x0, matrix products: 37.2 us -> none  [block_step(): exponent = jnp.exp(scores - row_max)]
    pallas_call x0 -> x1, Pallas kernels: none -> 27.8 us  [attend(): pl.pallas_call(functools.partial(attend_body, total, unroll), out_shape=(...]
    unnamed x4, waiting for transfers between devices: 21.2 us -> 0.73 us
  transfers between devices with their start and end apart: 5 -> 7, of which waited for: 4 -> 5; matrix products, arithmetic and copies ran while one was open for 5% -> 14% of each run, Pallas kernels for 0% -> 10%
where the time goes in v1:
time: 290 us; the launch traced here: 289 us
  waiting for transfers between devices  171 us (59%)
  Pallas kernels  27.8 us (10%)
  matrix products  26 us (9%)
  local copies, waits for them, and re-layouts  17.4 us (6%)
  blocking collectives  14.9 us (5%)
  starting transfers between devices  14.2 us (5%)
  between operations  13.9 us (5%)
  other arithmetic  4.43 us (2%)
    all_gather x1, waiting for transfers between devices, per_device(): normed_full = lax.all_gather(normed, 'seq', axis=0, tiled=True)  57.6 us
    reduce_scatter x1, waiting for transfers between devices, per_device(): owned = lax.psum_scatter(partial, 'fsdp', scatter_dimension=0, tiled=True)  54.2 us
    all_gather x1, waiting for transfers between devices, per_device(): lax.all_gather(own.reshape(rows, 3 * per_rank), 'fsdp', axis=0, tiled=True)  35.5 us
    pallas_call x1, Pallas kernels, attend(): pl.pallas_call(functools.partial(attend_body, total, unroll), out_shape=(...  27.8 us
    all_to_all x1, waiting for transfers between devices, per_device(): lax.all_to_all(grads.reshape(ranks, frame_count, 3 * per_rank), 'seq', 0,...  15 us
    all_gather x1, blocking collectives, per_device(): lax.all_gather(owned.reshape(rows, 3, per_rank), 'seq', axis=2, tiled=True)  14.9 us
    dot_general x1, matrix products, per_device(): lax.dot_general(normed_full, grads, (((0,), (0,)), ((), ())), preferred_e...  9.34 us
    dot_general x1, matrix products, per_device(): jnp.dot(normed_full, own_full, preferred_element_type=jnp.float32)  8.97 us
  transfers between devices with their start and end apart: 7, of which 5 were waited for; matrix products, arithmetic and copies ran while one was open for 14% of the time, Pallas kernels for 10%

profile of v1, /device:TPU:1, one launch (start us, length us, event | category | flops | bytes accessed | tf_op | source)
XLA Modules:
  0.0 289.3 jit_solution(2024529799392326582)
XLA Ops:
  7.2 1.9 reshape.57
  9.2 0.6 copy.19
  9.9 0.0 all-gather.4.cloned.1.call-start
  9.9 0.2 convert_reduce_fusion
  10.2 0.5 fusion.10
  10.7 1.4 fusion.5
  12.1 0.7 all-gather.8.cloned.1.call-update
  12.8 0.2 copy.14
  13.0 1.0 copy.18
  14.0 5.8 %all-to-all-start = ((bf16[8,384,128]{2,1,0:T(8,128)(2,1)}), bf16[8,384,128]{2,1,0:T(8,128)(2,1)S(1)}, u32[]{:S(2)}, u32[]{:S(2)}) async-start(bf16[8,384,128]{2,1,0:T(8,128)(2,1)} %bitcast.53), calls=%async_computation | async-start | bytes 1572864 | tf_op jit(solution)/shard_map/all_to_all | solution.py:117
  19.8 35.5 %all-gather.6.cloned.1.call-done = bf16[1536,384]{1,0:T(8,128)(2,1)} async-done(((bf16[96,384]{1,0:T(8,128)(2,1)}), bf16[1536,384]{1,0:T(8,128)(2,1)}) %all-gather.6.cloned.1.call-update) | async-done | bytes 1179664 | tf_op jit(solution)/shard_map/all_gather | solution.py:116
  55.3 57.6 %all-gather.4.cloned.1.call-done = bf16[3072,1536]{1,0:T(8,128)(2,1)} async-done(((bf16[384,1536]{1,0:T(8,128)(2,1)}), bf16[3072,1536]{1,0:T(8,128)(2,1)}) %all-gather.4.cloned.1.call-update) | async-done | bytes 9437200 | tf_op jit(solution)/shard_map/all_gather | solution.py:120
  112.8 9.0 %convolution_convert_fusion.qkv_ref = bf16[3072,384]{1,0:T(8,128)(2,1)} fusion(bf16[3072,1536]{1,0:T(8,128)(2,1)} %all-gather.4.cloned.1.call-done, bf16[1536,384]{1,0:T(8,128)(2,1)} %all-gather.6.cloned.1.call-done), kind=kOutput, calls=%fused_computation | convolution fusion | flops 3625058304 | bytes 12976128 | tf_op jit(solution)/shard_map/dot_general | solution.py:122
  121.8 0.9 copy-done.2
  122.7 27.8 %attention.1 = (bf16[3072,128]{1,0:T(8,128)(2,1)}, bf16[3072,384]{1,0:T(8,128)(2,1)}) custom-call(s32[12]{0:T(128)} %bitcast.67, bf16[3072,384]{1,0:T(8,128)(2,1)} %convolution_convert_fusion.qkv_ref, bf16[3072,128]{1,0:T(8,128)(2,1)} %bitcast.59), custom_call_target="tpu_custom_call" | custom-call | tf_op jit(solution)/shard_map/attention/pallas_call | solution.py:89
  150.5 3.7 %all-to-all-start.1 = ((bf16[8,384,128]{2,1,0:T(8,128)(2,1)}), bf16[8,384,128]{2,1,0:T(8,128)(2,1)S(1)}, u32[]{:S(2)}, u32[]{:S(2)}) async-start(bf16[8,384,128]{2,1,0:T(8,128)(2,1)} %bitcast.63), calls=%async_computation.1 | async-start | bytes 1572864 | tf_op jit(solution)/shard_map/all_to_all | solution.py:124
  154.2 4.3 %copy.11 = bf16[8,384,384]{1,2,0:T(8,128)(2,1)} copy(bf16[8,384,384]{2,1,0:T(8,128)(2,1)} %bitcast.60) | data formatting | bytes 4718592 | tf_op jit(solution)/shard_map/reshape | solution.py:125
  158.5 7.9 %all-to-all-done.1 = bf16[8,384,128]{2,1,0:T(8,128)(2,1)S(1)} async-done(((bf16[8,384,128]{2,1,0:T(8,128)(2,1)}), bf16[8,384,128]{2,1,0:T(8,128)(2,1)S(1)}, u32[]{:S(2)}, u32[]{:S(2)}) %all-to-all-start.1) | async-done | bytes 786464 | tf_op jit(solution)/shard_map/all_to_all | solution.py:124
  166.4 0.9 copy-done.1
  167.3 4.5 %all-to-all-start.2 = ((bf16[8,384,384]{1,2,0:T(8,128)(2,1)}), bf16[8,384,384]{1,2,0:T(8,128)(2,1)S(1)}, u32[]{:S(2)}, u32[]{:S(2)}) async-start(bf16[8,384,384]{1,2,0:T(8,128)(2,1)} %copy.11), calls=%async_computation.2 | async-start | bytes 4718592 | tf_op jit(solution)/shard_map/all_to_all | solution.py:125
  171.8 9.3 %convolution_convert_fusion.1 = bf16[1536,384]{1,0:T(8,128)(2,1)} fusion(bf16[3072,1536]{1,0:T(8,128)(2,1)} %all-gather.4.cloned.1.call-done, bf16[3072,384]{1,0:T(8,128)(2,1)} %get-tuple-element.6), kind=kOutput, calls=%fused_computation.3 | convolution fusion | flops 3624468480 | bytes 12976128 | tf_op jit(solution)/shard_map/dot_general | solution.py:126
  181.2 2.5 copy.10
  183.7 2.1 reshape.61
  185.8 15.0 %all-to-all-done.2 = bf16[8,384,384]{1,2,0:T(8,128)(2,1)S(1)} async-done(((bf16[8,384,384]{1,2,0:T(8,128)(2,1)}), bf16[8,384,384]{1,2,0:T(8,128)(2,1)S(1)}, u32[]{:S(2)}, u32[]{:S(2)}) %all-to-all-start.2) | async-done | bytes 2359328 | tf_op jit(solution)/shard_map/all_to_all | solution.py:125
  200.8 1.7 copy.12
  202.5 7.7 %fusion.12 = (f32[384]{0:T(512)S(1)}, f32[384]{0:T(512)S(1)}, f32[384,1536]{1,0:T(8,128)S(1)}) fusion(f32[384]{0:T(512)S(1)} %add_rsqrt_fusion, f32[384]{0:T(512)S(1)} %broadcast_multiply_fusion.2, bf16[1,384,1536]{2,1,0:T(8,128)(2,1)S(1)} %copy-done, bf16[384,3072]{0,1:T(8,128)(2,1)} %bitcast.61, bf16[1536,3072]{1,0:T(8,128)(2,1)} %all-gather.8.cloned.1.call-done), kind=kOutput, calls=%fused_computation.24 | convolution fusion | flops 3627416576 | bytes 15341568 | tf_op jit(solution)/shard_map/dot_general | solution.py:138
  210.2 1.7 fusion.11
  211.9 54.2 %reduce-scatter.2.cloned.1.call-done = bf16[96,384]{1,0:T(8,128)(2,1)} async-done(((bf16[1536,384]{1,0:T(8,128)(2,1)}), bf16[96,384]{1,0:T(8,128)(2,1)}) %reduce-scatter.2.cloned.1.call-update) | async-done | bytes 73744 | tf_op jit(solution)/shard_map/reduce_scatter | solution.py:129
  266.1 0.9 reshape.65
  267.0 14.9 %all_gather.15 = bf16[96,3,1024]{2,1,0:T(4,128)(2,1)S(1)} all-gather(bf16[96,3,128]{2,1,0:T(4,128)(2,1)S(1)} %reshape.65), channel_id=1, replica_groups=mesh['fsdp'=16,'seq'=8] {'seq'}, dimensions={2}, use_global_device_ids=true | all-gather | bytes 663552 | tf_op jit(solution)/shard_map/all_gather | solution.py:130
  281.9 0.3 copy.15
  282.1 0.7 dynamic-slice_convert_fusion
  (18 shorter events, 0.2 us)
Async XLA Ops:
  7.2 2.8 copy-start
  7.2 48.1 %all-gather.6.cloned.1.call-start = ((), (), s32[]{:S(2)}) async-start(), calls=%async_computation.5 | async-start | bytes 1253376 | tf_op jit(solution)/shard_map/all_gather | solution.py:116
  9.9 103.0 %all-gather.4.cloned.1.call-start = ((), (), s32[]{:S(2)}) async-start(), calls=%async_computation.4 | async-start | bytes 10616832 | tf_op jit(solution)/shard_map/all_gather | solution.py:120
  10.6 2.1 copy-start.3
  12.0 190.5 %all-gather.8.cloned.1.call-start = ((), (), s32[]{:S(2)}) async-start(), calls=%async_computation.6 | async-start | bytes 10027008 | tf_op jit(solution)/shard_map/all_gather | solution.py:121
  14.0 107.8 %all-to-all-start = ((bf16[8,384,128]{2,1,0:T(8,128)(2,1)}), bf16[8,384,128]{2,1,0:T(8,128)(2,1)S(1)}, u32[]{:S(2)}, u32[]{:S(2)}) async-start(bf16[8,384,128]{2,1,0:T(8,128)(2,1)} %bitcast.53), calls=%async_computation | async-start | bytes 1572864 | tf_op jit(solution)/shard_map/all_to_all | solution.py:117
  121.8 0.9 copy-start.2
  150.5 15.9 %all-to-all-start.1 = ((bf16[8,384,128]{2,1,0:T(8,128)(2,1)}), bf16[8,384,128]{2,1,0:T(8,128)(2,1)S(1)}, u32[]{:S(2)}, u32[]{:S(2)}) async-start(bf16[8,384,128]{2,1,0:T(8,128)(2,1)} %bitcast.63), calls=%async_computation.1 | async-start | bytes 1572864 | tf_op jit(solution)/shard_map/all_to_all | solution.py:124
  166.4 0.9 copy-start.1
  167.3 33.5 %all-to-all-start.2 = ((bf16[8,384,384]{1,2,0:T(8,128)(2,1)}), bf16[8,384,384]{1,2,0:T(8,128)(2,1)S(1)}, u32[]{:S(2)}, u32[]{:S(2)}) async-start(bf16[8,384,384]{1,2,0:T(8,128)(2,1)} %copy.11), calls=%async_computation.2 | async-start | bytes 4718592 | tf_op jit(solution)/shard_map/all_to_all | solution.py:125
  171.8 94.3 %reduce-scatter.2.cloned.1.call-start = ((), (), s32[]{:S(2)}) async-start(), calls=%async_computation.7 | async-start | bytes 1253376 | tf_op jit(solution)/shard_map/reduce_scatter | solution.py:129
Sparse Core Ops, SparseCore 0:
  10.7 44.4 all-gather.5
  57.5 55.2 all-gather.3
  115.0 75.5 all-gather.7
  193.7 72.3 reduce-scatter.1

commit v2 on v1

--- a/solution.py
+++ b/solution.py
@@ -97,53 +97,331 @@
     )(lengths, qkv, cot)
 
 
-def per_device(frames, lengths, w_qkv, d_context):
-    values_in = frames[0].astype(jnp.float32)
-    frame_count, model = values_in.shape
-    ranks = lax.axis_size("seq")
-    rank = lax.axis_index("seq")
-    total = frame_count * ranks
-    width = d_context.shape[2]
-    per_rank = width // ranks
+MESH = pl.DeviceIdType.MESH
+BF = jnp.bfloat16
+F32 = jnp.float32
+
+
+def place():
+    f = lax.axis_index("fsdp")
+    s = lax.axis_index("seq")
+    return f, s
+
+
+def greet(f, s, ranks, shards):
+    barrier = pltpu.get_barrier_semaphore()
+    for k in range(1, ranks):
+        pl.semaphore_signal(barrier, inc=1, device_id=(f, lax.rem(s + k, ranks)), device_id_type=MESH)
+    for k in range(1, shards):
+        pl.semaphore_signal(barrier, inc=1, device_id=(lax.rem(f + k, shards), s), device_id_type=MESH)
+    pl.semaphore_wait(barrier, ranks + shards - 2)
+
+
+def whiten(values_in):
     average = jnp.mean(values_in, axis=1, keepdims=True)
     centred = values_in - average
     variance = jnp.mean(centred * centred, axis=1, keepdims=True)
     inverse_scale = lax.rsqrt(variance + 1e-05)
-    whitened = centred * inverse_scale
-    normed = whitened.astype(jnp.bfloat16)
-    rows = w_qkv.shape[0]
-    own = lax.dynamic_slice_in_dim(w_qkv.reshape(rows, 3, width), rank * per_rank, per_rank, 2)
-    own_full = lax.all_gather(own.reshape(rows, 3 * per_rank), "fsdp", axis=0, tiled=True)
-    cot = lax.all_to_all(
-        d_context[0].reshape(frame_count, ranks, per_rank).transpose(1, 0, 2), "seq", 0, 0, tiled=True
-    ).reshape(total, per_rank)
-    normed_full = lax.all_gather(normed, "seq", axis=0, tiled=True)
-    weight_full = lax.all_gather(w_qkv, "fsdp", axis=0, tiled=True)
-    qkv = jnp.dot(normed_full, own_full, preferred_element_type=jnp.float32).astype(jnp.bfloat16)
+    return centred * inverse_scale, inverse_scale
+
+
+def front_body(ranks, shards, frames, cot_in, w_in, normed, qkv, cot, w_own, stage,
+               cot_send, cot_recv, w_send, w_recv, send, recv, local):
+    f, s = place()
+    rows = frames.shape[0]
+    half = rows // 2
+    chip, core = s // 2, lax.rem(s, 2)
+    chips = ranks // 2
+    right = lax.rem(chip + 1, chips) * 2 + core
+    left = lax.rem(chip + chips - 1, chips) * 2 + core
+    across = lax.rem(chip + 2, chips) * 2 + core
+    flip = 1 - 2 * core
+    partner = s + flip
+    depth = w_in.shape[0]
+    head = pl.ds(pl.multiple_of(s * 128, 128), 128)
+
+    parts = []
+    for t in range(3):
+        column = pl.multiple_of(t * ranks * 128 + s * 128, 128)
+        parts.append(pltpu.make_async_copy(w_in.at[:, pl.ds(column, 128)], stage.at[:, pl.ds(t * 128, 128)], local.at[t]))
+        parts[t].start()
+    greet(f, s, ranks, shards)
+
+    def block(rank, offset=0, count=rows):
+        return normed.at[pl.ds(pl.multiple_of(rank * rows + offset, 64), count)]
+
+    def move(role, rank, offset, count, target):
+        copy = pltpu.make_async_remote_copy(
+            src_ref=block(rank, offset, count), dst_ref=block(rank, offset, count),
+            send_sem=send.at[role], recv_sem=recv.at[role], device_id=(f, target), device_id_type=MESH)
+        copy.start()
+        started.append(copy)
+
+    def arrived(role, rank, offset, count):
+        pltpu.make_async_remote_copy(
+            src_ref=block(rank, offset, count), dst_ref=block(rank, offset, count),
+            send_sem=send.at[role], recv_sem=recv.at[role], device_id=(f, s), device_id_type=MESH).wait_recv()
+
+    started = []
+    cots = []
+    for k in (4, 3, 5, 2, 6, 1, 7):
+        d = lax.rem(s + k, ranks)
+        copy = pltpu.make_async_remote_copy(
+            src_ref=cot_in.at[:, pl.ds(pl.multiple_of(d * 128, 128), 128)],
+            dst_ref=cot.at[pl.ds(pl.multiple_of(s * rows, 128), rows)],
+            send_sem=cot_send.at[k], recv_sem=cot_recv.at[k], device_id=(f, d), device_id_type=MESH)
+        copy.start()
+        cots.append(copy)
+    for part in parts:
+        part.wait()
+    slices = []
+    for k in range(1, shards):
+        copy = pltpu.make_async_remote_copy(
+            src_ref=stage, dst_ref=w_own.at[pl.ds(pl.multiple_of(f * depth, 32), depth)],
+            send_sem=w_send.at[k], recv_sem=w_recv.at[k],
+            device_id=(lax.rem(f + k, shards), s), device_id_type=MESH)
+        copy.start()
+        slices.append(copy)
+
+    def norm(offset):
+        whitened, _ = whiten(frames[pl.ds(offset, half), :].astype(F32))
+        normed[pl.ds(pl.multiple_of(s * rows + offset, 64), half), :] = whitened.astype(BF)
+
+    norm(0)
+    move(0, s, 0, half, right)
+    norm(half)
+    move(2, s, half, half, left)
+    move(1, s, half, half, right)
+    move(3, s, 0, half, left)
+    move(6, s, 0, rows, partner)
+    cot[pl.ds(pl.multiple_of(s * rows, 128), rows), :] = cot_in[:, head]
+    w_own[pl.ds(pl.multiple_of(f * depth, 32), depth), :] = stage[...]
+
+    arrived(0, left, 0, half)
+    move(4, left, 0, half, right)
+    arrived(2, right, half, half)
+    move(5, right, half, half, left)
+
+    def project(rank):
+        def tile(i, _):
+            at = pl.ds(pl.multiple_of(rank * rows + i * half, 64), half)
+            qkv[at, :] = jnp.dot(normed[at, :], w_own[...], preferred_element_type=F32).astype(BF)
+            return 0
+        lax.fori_loop(0, 2, tile, 0)
+
+    for k in range(1, shards):
+        slices[k - 1].wait_recv()
+    project(s)
+    arrived(6, partner, 0, rows)
+    project(partner)
+    arrived(1, left, half, half)
+    move(7, left, 0, rows, partner)
+    arrived(3, right, 0, half)
+    move(8, right, 0, rows, partner)
+    project(left)
+    project(right)
+    arrived(7, left + flip, 0, rows)
+    project(left + flip)
+    arrived(8, right + flip, 0, rows)
+    project(right + flip)
+    arrived(4, across, 0, half)
+    move(9, across, 0, half, partner)
+    arrived(5, across, half, half)
+    move(10, across, half, half, partner)
+    project(across)
+    arrived(9, across + flip, 0, half)
+    arrived(10, across + flip, half, half)
+    project(across + flip)
+    for copy in cots:
+        copy.wait()
+    for copy in slices + started:
+        copy.wait_send()
+
+
+VM = pl.BlockSpec(memory_space=pltpu.VMEM)
+ANY = pl.BlockSpec(memory_space=pl.ANY)
+DMA = pltpu.SemaphoreType.DMA
+
+
+def front(ranks, shards, frames, cot_in, w_in):
+    rows, model = frames.shape
+    total = rows * ranks
+    return pl.pallas_call(
+        functools.partial(front_body, ranks, shards),
+        out_shape=(jax.ShapeDtypeStruct((total, model), BF), jax.ShapeDtypeStruct((total, 384), BF),
+                   jax.ShapeDtypeStruct((total, 128), BF)),
+        in_specs=[VM] * 3,
+        out_specs=(VM,) * 3,
+        scratch_shapes=[pltpu.VMEM((model, 384), BF), pltpu.VMEM((model // shards, 384), BF),
+                        DMA((ranks,)), DMA((ranks,)), DMA((shards,)), DMA((shards,)), DMA((11,)), DMA((11,)), DMA((3,))],
+        compiler_params=pltpu.CompilerParams(collective_id=0, has_side_effects=True, vmem_limit_bytes=40 * 2**20),
+        name="front",
+    )(frames, cot_in, w_in)
+
+
+def back_body(ranks, shards, ctx, grads, frames, normed_in, w_in, ctx_out, gi_out, gw_out,
+              normed, w, grads_t, got, part, shares, acc, white, scale, total_w,
+              g_send, g_recv, c_send, c_recv, r_send, r_recv, p_send, p_recv, local):
+    f, s = place()
+    rows, model = frames.shape
+    depth = model // shards
+    sides = 4
+    fy, fz = f // sides, lax.rem(f, sides)
+    load_n = pltpu.make_async_copy(normed_in, normed, local.at[0])
+    load_w = pltpu.make_async_copy(w_in, w, local.at[1])
+    load_n.start()
+    load_w.start()
+    greet(f, s, ranks, shards)
+    order = (1, 7, 2, 6, 3, 5, 4)
+    sent = {}
+    for k in order:
+        d = lax.rem(s + k, ranks)
+        theirs = pl.ds(pl.multiple_of(d * rows, 128), rows)
+        sent[k] = (
+            pltpu.make_async_remote_copy(
+                src_ref=grads.at[theirs], dst_ref=got.at[k], send_sem=g_send.at[k], recv_sem=g_recv.at[k],
+                device_id=(f, d), device_id_type=MESH),
+            pltpu.make_async_remote_copy(
+                src_ref=ctx.at[theirs], dst_ref=ctx_out.at[:, pl.ds(pl.multiple_of(s * 128, 128), 128)],
+                send_sem=c_send.at[k], recv_sem=c_recv.at[k], device_id=(f, d), device_id_type=MESH))
+        for copy in sent[k]:
+            copy.start()
+    mine = pl.ds(pl.multiple_of(s * rows, 128), rows)
+    ctx_out[:, pl.ds(pl.multiple_of(s * 128, 128), 128)] = ctx[mine, :]
+
+    def turn(i, _):
+        at = pl.ds(pl.multiple_of(i * 128, 128), 128)
+        grads_t[:, at] = grads[at, :].T
+        return 0
+
+    lax.fori_loop(0, grads.shape[0] // 128, turn, 0)
+    load_n.wait()
+    group = depth * sides
+    shared = []
+    for j in (1, 2, 3, 0):
+        y = lax.rem(fy + j, sides)
+        at = pl.ds(pl.multiple_of(y * group, 128), group)
+        product = jnp.dot(grads_t[...], normed[:, at], preferred_element_type=F32)
+        part[at, :] = product.T.astype(BF)
+        for k in (1, 2, 3, 0):
+            if j == 0 and k == 0:
+                continue
+            peer = y * sides + lax.rem(fz + k, sides)
+            copy = pltpu.make_async_remote_copy(
+                src_ref=part.at[pl.ds(pl.multiple_of(peer * depth, 32), depth)], dst_ref=shares.at[4 * j + k],
+                send_sem=r_send.at[4 * j + k], recv_sem=r_recv.at[4 * j + k],
+                device_id=(peer, s), device_id_type=MESH)
+            copy.start()
+            shared.append(copy)
+
+    def prepare(i, _):
+        at = pl.ds(pl.multiple_of(i * depth, 32), depth)
+        whitened, inverse_scale = whiten(frames[at, :].astype(F32))
+        white[at, :] = whitened
+        scale[at, :] = jnp.broadcast_to(inverse_scale, (depth, 128))
+        return 0
+
+    lax.fori_loop(0, rows // depth, prepare, 0)
+    load_w.wait()
+
+    def pull(block, rank):
+        return lax.dot_general(block, w[rank], NT, preferred_element_type=F32)
+
+    acc[...] = pull(grads[mine, :], s)
+    for k in order[:4]:
+        sent[k][0].wait_recv()
+        acc[...] += pull(got[k], lax.rem(s + ranks - k, ranks))
+    for copy in shared:
+        copy.wait_recv()
+    sums = part[pl.ds(pl.multiple_of(f * depth, 32), depth), :].astype(F32)
+    for k in range(1, shards):
+        sums += shares[k].astype(F32)
+    total_w[...] = sums
+    for t in range(3):
+        number = t * ranks + s
+        owner, slot = number // 3, lax.rem(number, 3)
+        source = total_w.at[:, pl.ds(t * 128, 128)]
+        target = gw_out.at[:, pl.ds(pl.multiple_of(slot * 128, 128), 128)]
+
+        @pl.when(owner != s)
+        def _():
+            pltpu.make_async_remote_copy(
+                src_ref=source, dst_ref=target, send_sem=p_send.at[t], recv_sem=p_recv.at[slot],
+                device_id=(f, owner), device_id_type=MESH).start()
+
+        @pl.when(owner == s)
+        def _():
+            target[...] = sums[:, t * 128:t * 128 + 128]
+
+    for k in order[4:]:
+        sent[k][0].wait_recv()
+        acc[...] += pull(got[k], lax.rem(s + ranks - k, ranks))
+
+    def finish(i, _):
+        at = pl.ds(pl.multiple_of(i * depth, 32), depth)
+        gn = acc[at, :]
+        whitened = white[at, :]
+        inner = jnp.mean(gn * whitened, axis=1, keepdims=True)
+        out = scale[at, 0:1] * (gn - jnp.mean(gn, axis=1, keepdims=True) - whitened * inner)
+        gi_out[at, :] = out.astype(BF)
+        return 0
+
+    lax.fori_loop(0, rows // depth, finish, 0)
+    for slot in range(3):
+        source_rank = lax.rem(3 * s + slot, ranks)
+
+        @pl.when(source_rank != s)
+        def _():
+            pltpu.make_async_remote_copy(
+                src_ref=total_w.at[:, pl.ds(0, 128)], dst_ref=gw_out.at[:, pl.ds(slot * 128, 128)],
+                send_sem=p_send.at[slot], recv_sem=p_recv.at[slot], device_id=(f, s), device_id_type=MESH).wait_recv()
+
+    for t in range(3):
+        owner = (t * ranks + s) // 3
+
+        @pl.when(owner != s)
+        def _():
+            pltpu.make_async_remote_copy(
+                src_ref=total_w.at[:, pl.ds(t * 128, 128)], dst_ref=gw_out.at[:, pl.ds(0, 128)],
+                send_sem=p_send.at[t], recv_sem=p_recv.at[t], device_id=(f, owner), device_id_type=MESH).wait_send()
+
+    for k in order:
+        sent[k][0].wait_send()
+        sent[k][1].wait()
+    for copy in shared:
+        copy.wait_send()
+
+
+def back(ranks, shards, ctx, grads, frames, normed, w):
+    rows, model = frames.shape
+    total = rows * ranks
+    depth = model // shards
+    return pl.pallas_call(
+        functools.partial(back_body, ranks, shards),
+        out_shape=(jax.ShapeDtypeStruct((rows, ranks * 128), BF), jax.ShapeDtypeStruct((rows, model), BF),
+                   jax.ShapeDtypeStruct((depth, 384), F32)),
+        in_specs=[VM] * 3 + [ANY] * 2,
+        out_specs=(VM,) * 3,
+        scratch_shapes=[
+            pltpu.VMEM((total, model), BF), pltpu.VMEM((ranks, model, 384), BF), pltpu.VMEM((384, total), BF),
+            pltpu.VMEM((ranks, rows, 384), BF), pltpu.VMEM((model, 384), BF), pltpu.VMEM((shards, depth, 384), BF),
+            pltpu.VMEM((rows, model), F32), pltpu.VMEM((rows, model), F32), pltpu.VMEM((rows, 128), F32),
+            pltpu.VMEM((depth, 384), F32)]
+        + [DMA((ranks,))] * 4 + [DMA((shards,))] * 2 + [DMA((3,))] * 2 + [DMA((2,))],
+        compiler_params=pltpu.CompilerParams(collective_id=1, has_side_effects=True, vmem_limit_bytes=60 * 2**20),
+        name="back",
+    )(ctx, grads, frames, normed, w)
+
+
+def per_device(frames, lengths, w_qkv, d_context):
+    ranks, shards = lax.axis_size("seq"), lax.axis_size("fsdp")
+    depth, model = w_qkv.shape[0], frames.shape[2]
+    by_owner = w_qkv.reshape(depth, 3, ranks, 128).transpose(2, 0, 1, 3).reshape(ranks, depth, 384)
+    weight_full = lax.all_gather(by_owner, "fsdp", axis=1, tiled=True)
+    normed, qkv, cot = front(ranks, shards, frames[0], d_context[0], w_qkv)
     context, grads = attend(lengths[0], qkv, cot, 5)
-    context_back = lax.all_to_all(context.reshape(ranks, frame_count, per_rank), "seq", 0, 0, tiled=True)
-    grads_back = lax.all_to_all(grads.reshape(ranks, frame_count, 3 * per_rank), "seq", 0, 0, tiled=True)
-    partial = lax.dot_general(
-        normed_full, grads, (((0,), (0,)), ((), ())), preferred_element_type=jnp.float32
-    ).astype(jnp.bfloat16)
-    owned = lax.psum_scatter(partial, "fsdp", scatter_dimension=0, tiled=True)
-    blocks = lax.all_gather(owned.reshape(rows, 3, per_rank), "seq", axis=2, tiled=True)
-    grad_weight = lax.dynamic_slice_in_dim(
-        blocks.reshape(rows, 3 * width), rank * 3 * per_rank, 3 * per_rank, 1
-    ).astype(jnp.float32)
-    context_out = context_back.transpose(1, 0, 2).reshape(1, frame_count, width)
-    grad_qkv = (
-        grads_back.reshape(ranks, frame_count, 3, per_rank).transpose(1, 2, 0, 3).reshape(frame_count, 3 * width)
-    )
-    grad_normed = lax.dot_general(
-        grad_qkv, weight_full, (((1,), (1,)), ((), ())), preferred_element_type=jnp.float32
-    )
-    grad_input = inverse_scale * (
-        grad_normed
-        - jnp.mean(grad_normed, axis=1, keepdims=True)
-        - whitened * jnp.mean(grad_normed * whitened, axis=1, keepdims=True)
-    )
-    return context_out, grad_input.astype(jnp.bfloat16)[None], grad_weight
+    context_out, grad_input, grad_weight = back(ranks, shards, context, grads, frames[0], normed, weight_full)
+    return context_out[None], grad_input[None], grad_weight
 
 
 def solution(mesh):

time: 290 us -> 160 us (0.55)
  waiting for transfers between devices: 171 us -> 0.02 us
  Pallas kernels: 27.8 us -> 137 us
  matrix products: 26 us -> 0 us
  blocking collectives: 14.9 us -> 0 us
  starting transfers between devices: 14.2 us -> 0.04 us
  local copies, waits for them, and re-layouts: 17.4 us -> 9.08 us
  other arithmetic: 4.43 us -> 0 us
    pallas_call x0 -> x2, Pallas kernels: none -> 111 us  [the longest x1 65.5 us: front(): pl.pallas_call(functools.partial(front_body, ranks, shards), out_shape=(j...]
    all_gather x3 -> x1, waiting for transfers between devices: 93.1 us -> 0.01 us  [per_device(): weight_full = lax.all_gather(by_owner, 'fsdp', axis=1, tiled=True)]
    reduce_scatter x1 -> x0, waiting for transfers between devices: 54.2 us -> none  [per_device(): owned = lax.psum_scatter(partial, 'fsdp', scatter_dimension=0, tiled=True)]
    dot_general x3 -> x0, matrix products: 26 us -> none  [the longest x1 9.34 us: per_device(): lax.dot_general(normed_full, grads, (((0,), (0,)), ((), ())), preferred_e...]
    all_to_all x3 -> x0, waiting for transfers between devices: 22.9 us -> none  [the longest x1 15 us: per_device(): lax.all_to_all(grads.reshape(ranks, frame_count, 3 * per_rank), 'seq', 0,...]
    all_gather x1 -> x0, blocking collectives: 14.9 us -> none  [per_device(): lax.all_gather(owned.reshape(rows, 3, per_rank), 'seq', axis=2, tiled=True)]
    all_to_all x3 -> x0, starting transfers between devices: 14 us -> none  [the longest x1 5.79 us: per_device(): lax.all_to_all(d_context[0].reshape(frame_count, ranks, per_rank).transpo...]
    reshape x4 -> x2, local copies, waits for them, and re-layouts: 9.28 us -> 1.57 us  [per_device(): w_qkv.reshape(depth, 3, ranks, 128).transpose(2, 0, 1, 3)]
  transfers between devices with their start and end apart: 7 -> 1, of which waited for: 5 -> 0; matrix products, arithmetic and copies ran while one was open for 14% -> 0% of each run, Pallas kernels for 10% -> 57%
where the time goes in v2:
time: 160 us
  Pallas kernels  137 us (86%)
  between operations  14.1 us (9%)
  local copies, waits for them, and re-layouts  9.08 us (6%)
    pallas_call x1, Pallas kernels, front(): pl.pallas_call(functools.partial(front_body, ranks, shards), out_shape=(j...  65.5 us
    pallas_call x1, Pallas kernels, back(): pl.pallas_call(functools.partial(back_body, ranks, shards), out_shape=(ja...  45.5 us
    pallas_call x1, Pallas kernels, attend(): pl.pallas_call(functools.partial(attend_body, total, unroll), out_shape=(...  25.5 us
    unnamed x18, local copies, waits for them, and re-layouts  7.51 us
  transfers between devices with their start and end apart: 1, of which 0 were waited for; matrix products, arithmetic and copies ran while one was open for 0% of the time, Pallas kernels for 57%

profile of v2, /device:TPU:1, one launch (start us, length us, event | category | flops | bytes accessed | tf_op | source)
XLA Modules:
  0.0 159.8 jit_solution(13095102949450604673)
XLA Ops:
  7.2 0.0 copy-start.1
  7.2 0.0 copy-start
  7.2 0.0 copy-start.3
  7.2 0.0 all-gather.2.cloned.1.call-start
  7.2 1.3 copy.9
  8.6 0.3 copy.11
  8.9 1.3 reshape.13
  10.1 0.0 all-gather.2.cloned.1.call-update
  10.2 0.0 copy-done.1
  10.2 0.0 copy-done
  10.2 0.0 copy-done.3
  10.2 65.5 %front.1 = (bf16[3072,1536]{1,0:T(8,128)(2,1)}, bf16[3072,384]{1,0:T(8,128)(2,1)S(1)}, bf16[3072,128]{1,0:T(8,128)(2,1)S(1)}) custom-call(bf16[384,1536]{1,0:T(8,128)(2,1)S(1)} %bitcast.12, bf16[384,1024]{1,0:T(8,128)(2,1)S(1)} %bitcast.14, bf16[96,3072]{1,0:T(8,128)(2,1)S(1)} %copy-done.1), custom_call_target="tpu_custom_call" | custom-call | tf_op jit(solution)/shard_map/front/pallas_call | solution.py:249
  75.8 0.0 copy-start.2
  75.8 1.4 copy-done.2
  77.2 0.0 copy-start.4
  77.2 0.9 copy-done.4
  78.1 25.5 %attention.1 = (bf16[3072,128]{1,0:T(8,128)(2,1)}, bf16[3072,384]{1,0:T(8,128)(2,1)}) custom-call(s32[12]{0:T(128)} %bitcast.19, bf16[3072,384]{1,0:T(8,128)(2,1)} %copy-done.2, bf16[3072,128]{1,0:T(8,128)(2,1)} %copy-done.4), custom_call_target="tpu_custom_call" | custom-call | tf_op jit(solution)/shard_map/attention/pallas_call | solution.py:89
  103.6 0.0 all-gather.2.cloned.1.call-done.w_in
  103.6 45.5 %back.1 = (bf16[384,1024]{1,0:T(8,128)(2,1)}, bf16[384,1536]{1,0:T(8,128)(2,1)}, f32[96,384]{1,0:T(8,128)}) custom-call(bf16[3072,128]{1,0:T(8,128)(2,1)} %get-tuple-element.13.ctx, bf16[3072,384]{1,0:T(8,128)(2,1)} %get-tuple-element.14.grads, bf16[384,1536]{1,0:T(8,128)(2,1)} %bitcast.11, bf16[3072,1536]{1,0:T(8,128)(2,1)} %get-tuple-element.15.normed_in, ...), custom_call_target="tpu_custom_call" | custom-call | tf_op jit(solution)/shard_map/back/pallas_call | solution.py:399
  149.1 0.0 copy-start.5
  149.1 0.0 copy-start.6
  149.1 2.2 %copy.15 = bf16[1,384,1024]{2,1,0:T(8,128)(2,1)} copy(bf16[1,384,1024]{2,1,0:T(8,128)(2,1)} %bitcast.18) | data formatting | bytes 1572864
  151.3 0.0 copy-done.5
  151.3 1.0 copy.16
  152.3 0.0 copy-done.6
  152.3 0.7 copy.17
Async XLA Ops:
  7.2 3.0 %copy-start.1 = (bf16[96,3072]{1,0:T(8,128)(2,1)S(1)}, bf16[96,3072]{1,0:T(8,128)(2,1)}, u32[]{:S(2)}) copy-start(bf16[96,3072]{1,0:T(8,128)(2,1)} %w_in.1) | copy-start | bytes 1769476
  7.2 3.0 %copy-start = (bf16[1,384,1536]{2,1,0:T(8,128)(2,1)S(1)}, bf16[1,384,1536]{2,1,0:T(8,128)(2,1)}, u32[]{:S(2)}) copy-start(bf16[1,384,1536]{2,1,0:T(8,128)(2,1)} %param.4) | copy-start | bytes 3538948
  7.2 3.0 %copy-start.3 = (bf16[1,384,1024]{2,1,0:T(8,128)(2,1)S(1)}, bf16[1,384,1024]{2,1,0:T(8,128)(2,1)}, u32[]{:S(2)}) copy-start(bf16[1,384,1024]{2,1,0:T(8,128)(2,1)} %param.7) | copy-start | bytes 2359300
  7.2 96.4 %all-gather.2.cloned.1.call-start = ((), (), s32[]{:S(2)}) async-start(), calls=%async_computation | async-start | bytes 10027008 | tf_op jit(solution)/shard_map/all_gather | solution.py:420
  75.8 1.5 copy-start.2
  77.2 0.9 copy-start.4
  149.1 2.2 %copy-start.5 = (bf16[384,1536]{1,0:T(8,128)(2,1)S(1)}, bf16[384,1536]{1,0:T(8,128)(2,1)}, u32[]{:S(2)}) copy-start(bf16[384,1536]{1,0:T(8,128)(2,1)} %get-tuple-element.17) | copy-start | bytes 3538948
  149.1 3.2 %copy-start.6 = (f32[96,384]{1,0:T(8,128)S(1)}, f32[96,384]{1,0:T(8,128)}, u32[]{:S(2)}) copy-start(f32[96,384]{1,0:T(8,128)} %get-tuple-element.24) | copy-start | bytes 442372
Sparse Core Ops, SparseCore 0:
  10.3 85.1 all-gather.1

commit v3 on v2

--- a/solution.py
+++ b/solution.py
@@ -93,6 +93,7 @@
         in_specs=[pl.BlockSpec(memory_space=pltpu.SMEM)] + [pl.BlockSpec(memory_space=pltpu.VMEM)] * 2,
         out_specs=(pl.BlockSpec(memory_space=pltpu.VMEM),) * 2,
         scratch_shapes=[pltpu.VMEM((128, 640), jnp.float32)] * 2,
+        compiler_params=pltpu.CompilerParams(vmem_limit_bytes=12 * 2**20),
         name="attention",
     )(lengths, qkv, cot)
 
@@ -125,44 +126,57 @@
     return centred * inverse_scale, inverse_scale
 
 
-def front_body(ranks, shards, frames, cot_in, w_in, normed, qkv, cot, w_own, stage,
-               cot_send, cot_recv, w_send, w_recv, send, recv, local):
+def front_body(ranks, shards, frames_in, cot_in, w_in, normed, qkv, cot, w, frames,
+               cot_send, cot_recv, one_send, one_recv, two_send, two_recv, mate_send, mate_recv, send, recv, local):
     f, s = place()
     rows = frames.shape[0]
     half = rows // 2
     chip, core = s // 2, lax.rem(s, 2)
     chips = ranks // 2
+    sides = w.shape[2]
+    fy, fz = f // sides, lax.rem(f, sides)
     right = lax.rem(chip + 1, chips) * 2 + core
     left = lax.rem(chip + chips - 1, chips) * 2 + core
     across = lax.rem(chip + 2, chips) * 2 + core
     flip = 1 - 2 * core
     partner = s + flip
-    depth = w_in.shape[0]
     head = pl.ds(pl.multiple_of(s * 128, 128), 128)
 
-    parts = []
-    for t in range(3):
-        column = pl.multiple_of(t * ranks * 128 + s * 128, 128)
-        parts.append(pltpu.make_async_copy(w_in.at[:, pl.ds(column, 128)], stage.at[:, pl.ds(t * 128, 128)], local.at[t]))
-        parts[t].start()
+    pieces = []
+    for i in range(chips):
+        for t in range(3):
+            column = pl.multiple_of((t * ranks + 2 * i + core) * 128, 128)
+            pieces.append(pltpu.make_async_copy(
+                w_in.at[:, pl.ds(column, 128)], w.at[i, core, fy, fz, :, pl.ds(t * 128, 128)], local.at[i * 3 + t]))
+            pieces[-1].start()
+    load_x = pltpu.make_async_copy(frames_in, frames, local.at[3 * chips])
+    load_x.start()
+    own_cot = pltpu.make_async_copy(
+        cot_in.at[:, head], cot.at[pl.ds(pl.multiple_of(s * rows, 128), rows)], local.at[3 * chips + 1])
+    own_cot.start()
     greet(f, s, ranks, shards)
+
+    started = []
+
+    def remote(ref, sends, recvs, role, target):
+        return pltpu.make_async_remote_copy(
+            src_ref=ref, dst_ref=ref, send_sem=sends.at[role], recv_sem=recvs.at[role],
+            device_id=target, device_id_type=MESH)
+
+    def push(ref, sends, recvs, role, target):
+        copy = remote(ref, sends, recvs, role, target)
+        copy.start()
+        started.append(copy)
 
     def block(rank, offset=0, count=rows):
         return normed.at[pl.ds(pl.multiple_of(rank * rows + offset, 64), count)]
 
     def move(role, rank, offset, count, target):
-        copy = pltpu.make_async_remote_copy(
-            src_ref=block(rank, offset, count), dst_ref=block(rank, offset, count),
-            send_sem=send.at[role], recv_sem=recv.at[role], device_id=(f, target), device_id_type=MESH)
-        copy.start()
-        started.append(copy)
+        push(block(rank, offset, count), send, recv, role, (f, target))
 
     def arrived(role, rank, offset, count):
-        pltpu.make_async_remote_copy(
-            src_ref=block(rank, offset, count), dst_ref=block(rank, offset, count),
-            send_sem=send.at[role], recv_sem=recv.at[role], device_id=(f, s), device_id_type=MESH).wait_recv()
-
-    started = []
+        remote(block(rank, offset, count), send, recv, role, (f, s)).wait_recv()
+
     cots = []
     for k in (4, 3, 5, 2, 6, 1, 7):
         d = lax.rem(s + k, ranks)
@@ -172,21 +186,26 @@
             send_sem=cot_send.at[k], recv_sem=cot_recv.at[k], device_id=(f, d), device_id_type=MESH)
         copy.start()
         cots.append(copy)
-    for part in parts:
-        part.wait()
-    slices = []
-    for k in range(1, shards):
-        copy = pltpu.make_async_remote_copy(
-            src_ref=stage, dst_ref=w_own.at[pl.ds(pl.multiple_of(f * depth, 32), depth)],
-            send_sem=w_send.at[k], recv_sem=w_recv.at[k],
-            device_id=(lax.rem(f + k, shards), s), device_id_type=MESH)
-        copy.start()
-        slices.append(copy)
+    for piece in pieces:
+        piece.wait()
+
+    def along(axis, step):
+        if axis == 0:
+            return lax.rem(fy + step, sides) * sides + fz
+        return fy * sides + lax.rem(fz + step, sides)
+
+    def shard(pair, peer):
+        return w.at[pl.ds(2 * pair, 2), core, peer // sides, lax.rem(peer, sides)]
+
+    for k in (2, 1, 3):
+        for pair in range(2):
+            push(shard(pair, f), one_send, one_recv, 4 * pair + k, (along(1 - pair, k), s))
 
     def norm(offset):
         whitened, _ = whiten(frames[pl.ds(offset, half), :].astype(F32))
         normed[pl.ds(pl.multiple_of(s * rows + offset, 64), half), :] = whitened.astype(BF)
 
+    load_x.wait()
     norm(0)
     move(0, s, 0, half, right)
     norm(half)
@@ -194,23 +213,57 @@
     move(1, s, half, half, right)
     move(3, s, 0, half, left)
     move(6, s, 0, rows, partner)
-    cot[pl.ds(pl.multiple_of(s * rows, 128), rows), :] = cot_in[:, head]
-    w_own[pl.ds(pl.multiple_of(f * depth, 32), depth), :] = stage[...]
+    own_cot.wait()
+
+    def line(pair, index, step):
+        i = 2 * pair + index
+        if pair == 0:
+            return w.at[i, core, lax.rem(fy + step, sides)]
+        return w.at[i, core, :, lax.rem(fz + step, sides)]
+
+    def pass_on(role, pair, index, step, toward):
+        push(line(pair, index, step), two_send, two_recv, 6 * pair + role, (along(pair, toward), s))
+
+    def come(role, pair, index, step):
+        remote(line(pair, index, step), two_send, two_recv, 6 * pair + role, (f, s)).wait_recv()
+
+    up, down = 1, sides - 1
+    for pair in range(2):
+        for k in (1, 3, 2):
+            peer = along(1 - pair, sides - k)
+            remote(shard(pair, peer), one_send, one_recv, 4 * pair + k, (f, s)).wait_recv()
+        pass_on(0, pair, 0, 0, up)
+        pass_on(1, pair, 1, 0, down)
+        pass_on(2, pair, 1, 0, up)
+        pass_on(3, pair, 0, 0, down)
+    for pair in range(2):
+        come(0, pair, 0, down)
+        pass_on(4, pair, 0, down, up)
+        come(1, pair, 1, up)
+        pass_on(5, pair, 1, up, down)
 
     arrived(0, left, 0, half)
     move(4, left, 0, half, right)
     arrived(2, right, half, half)
     move(5, right, half, half, left)
 
+    for pair in range(2):
+        come(2, pair, 1, down)
+        come(3, pair, 0, up)
+        come(4, pair, 0, 2)
+        come(5, pair, 1, 2)
+        push(w.at[pl.ds(2 * pair, 2), core], mate_send, mate_recv, pair, (f, partner))
+
+    mine = s // 2
+
     def project(rank):
         def tile(i, _):
             at = pl.ds(pl.multiple_of(rank * rows + i * half, 64), half)
-            qkv[at, :] = jnp.dot(normed[at, :], w_own[...], preferred_element_type=F32).astype(BF)
+            weight = w[mine, core].reshape(w.shape[2] * w.shape[3] * w.shape[4], w.shape[5])
+            qkv[at, :] = jnp.dot(normed[at, :], weight, preferred_element_type=F32).astype(BF)
             return 0
         lax.fori_loop(0, 2, tile, 0)
 
-    for k in range(1, shards):
-        slices[k - 1].wait_recv()
     project(s)
     arrived(6, partner, 0, rows)
     project(partner)
@@ -224,6 +277,8 @@
     project(left + flip)
     arrived(8, right + flip, 0, rows)
     project(right + flip)
+    for pair in range(2):
+        remote(w.at[pl.ds(2 * pair, 2), 1 - core], mate_send, mate_recv, pair, (f, s)).wait_recv()
     arrived(4, across, 0, half)
     move(9, across, 0, half, partner)
     arrived(5, across, half, half)
@@ -234,43 +289,46 @@
     project(across + flip)
     for copy in cots:
         copy.wait()
-    for copy in slices + started:
+    for copy in started:
         copy.wait_send()
 
 
 VM = pl.BlockSpec(memory_space=pltpu.VMEM)
-ANY = pl.BlockSpec(memory_space=pl.ANY)
+HBM = pl.BlockSpec(memory_space=pltpu.HBM)
+FRONT_MB = 8
+BACK_MB = 22
 DMA = pltpu.SemaphoreType.DMA
 
 
 def front(ranks, shards, frames, cot_in, w_in):
     rows, model = frames.shape
     total = rows * ranks
+    sides = 4
+    weight = (ranks // 2, 2, sides, shards // sides, w_in.shape[0], 384)
     return pl.pallas_call(
         functools.partial(front_body, ranks, shards),
         out_shape=(jax.ShapeDtypeStruct((total, model), BF), jax.ShapeDtypeStruct((total, 384), BF),
-                   jax.ShapeDtypeStruct((total, 128), BF)),
-        in_specs=[VM] * 3,
-        out_specs=(VM,) * 3,
-        scratch_shapes=[pltpu.VMEM((model, 384), BF), pltpu.VMEM((model // shards, 384), BF),
-                        DMA((ranks,)), DMA((ranks,)), DMA((shards,)), DMA((shards,)), DMA((11,)), DMA((11,)), DMA((3,))],
-        compiler_params=pltpu.CompilerParams(collective_id=0, has_side_effects=True, vmem_limit_bytes=40 * 2**20),
+                   jax.ShapeDtypeStruct((total, 128), BF), jax.ShapeDtypeStruct(weight, BF)),
+        in_specs=[HBM] * 3,
+        out_specs=(VM,) * 4,
+        scratch_shapes=[pltpu.VMEM((rows, model), BF),
+                        DMA((ranks,)), DMA((ranks,)), DMA((8,)), DMA((8,)), DMA((12,)), DMA((12,)), DMA((2,)), DMA((2,)),
+                        DMA((11,)), DMA((11,)), DMA((3 * ranks // 2 + 2,))],
+        compiler_params=pltpu.CompilerParams(collective_id=0, has_side_effects=True, vmem_limit_bytes=FRONT_MB * 2**20),
         name="front",
     )(frames, cot_in, w_in)
 
 
-def back_body(ranks, shards, ctx, grads, frames, normed_in, w_in, ctx_out, gi_out, gw_out,
-              normed, w, grads_t, got, part, shares, acc, white, scale, total_w,
+def back_body(ranks, shards, ctx, grads, frames_in, normed, w, ctx_out, gi_out, gw_out,
+              frames, grads_t, got, part, shares, acc, white, scale, total_w,
               g_send, g_recv, c_send, c_recv, r_send, r_recv, p_send, p_recv, local):
     f, s = place()
-    rows, model = frames.shape
+    rows, model = frames_in.shape
     depth = model // shards
     sides = 4
     fy, fz = f // sides, lax.rem(f, sides)
-    load_n = pltpu.make_async_copy(normed_in, normed, local.at[0])
-    load_w = pltpu.make_async_copy(w_in, w, local.at[1])
-    load_n.start()
-    load_w.start()
+    load_x = pltpu.make_async_copy(frames_in, frames, local.at[0])
+    load_x.start()
     greet(f, s, ranks, shards)
     order = (1, 7, 2, 6, 3, 5, 4)
     sent = {}
@@ -295,7 +353,6 @@
         return 0
 
     lax.fori_loop(0, grads.shape[0] // 128, turn, 0)
-    load_n.wait()
     group = depth * sides
     shared = []
     for j in (1, 2, 3, 0):
@@ -321,8 +378,8 @@
         scale[at, :] = jnp.broadcast_to(inverse_scale, (depth, 128))
         return 0
 
+    load_x.wait()
     lax.fori_loop(0, rows // depth, prepare, 0)
-    load_w.wait()
 
     def pull(block, rank):
         return lax.dot_general(block, w[rank], NT, preferred_element_type=F32)
@@ -400,27 +457,26 @@
         functools.partial(back_body, ranks, shards),
         out_shape=(jax.ShapeDtypeStruct((rows, ranks * 128), BF), jax.ShapeDtypeStruct((rows, model), BF),
                    jax.ShapeDtypeStruct((depth, 384), F32)),
-        in_specs=[VM] * 3 + [ANY] * 2,
+        in_specs=[VM] * 2 + [HBM] + [VM] * 2,
         out_specs=(VM,) * 3,
         scratch_shapes=[
-            pltpu.VMEM((total, model), BF), pltpu.VMEM((ranks, model, 384), BF), pltpu.VMEM((384, total), BF),
+            pltpu.VMEM((rows, model), BF), pltpu.VMEM((384, total), BF),
             pltpu.VMEM((ranks, rows, 384), BF), pltpu.VMEM((model, 384), BF), pltpu.VMEM((shards, depth, 384), BF),
             pltpu.VMEM((rows, model), F32), pltpu.VMEM((rows, model), F32), pltpu.VMEM((rows, 128), F32),
             pltpu.VMEM((depth, 384), F32)]
-        + [DMA((ranks,))] * 4 + [DMA((shards,))] * 2 + [DMA((3,))] * 2 + [DMA((2,))],
-        compiler_params=pltpu.CompilerParams(collective_id=1, has_side_effects=True, vmem_limit_bytes=60 * 2**20),
+        + [DMA((ranks,))] * 4 + [DMA((shards,))] * 2 + [DMA((3,))] * 2 + [DMA((1,))],
+        compiler_params=pltpu.CompilerParams(collective_id=1, has_side_effects=True, vmem_limit_bytes=BACK_MB * 2**20),
         name="back",
     )(ctx, grads, frames, normed, w)
 
 
 def per_device(frames, lengths, w_qkv, d_context):
     ranks, shards = lax.axis_size("seq"), lax.axis_size("fsdp")
-    depth, model = w_qkv.shape[0], frames.shape[2]
-    by_owner = w_qkv.reshape(depth, 3, ranks, 128).transpose(2, 0, 1, 3).reshape(ranks, depth, 384)
-    weight_full = lax.all_gather(by_owner, "fsdp", axis=1, tiled=True)
-    normed, qkv, cot = front(ranks, shards, frames[0], d_context[0], w_qkv)
+    model = frames.shape[2]
+    normed, qkv, cot, weight_full = front(ranks, shards, frames[0], d_context[0], w_qkv)
     context, grads = attend(lengths[0], qkv, cot, 5)
-    context_out, grad_input, grad_weight = back(ranks, shards, context, grads, frames[0], normed, weight_full)
+    context_out, grad_input, grad_weight = back(
+        ranks, shards, context, grads, frames[0], normed, weight_full.reshape(ranks, model, 384))
     return context_out[None], grad_input[None], grad_weight
 
 

time: 160 us -> 134 us (0.84)
  between operations: 14.1 us -> 0.69 us
  Pallas kernels: 137 us -> 127 us
  local copies, waits for them, and re-layouts: 9.08 us -> 6.03 us
    pallas_call x1, Pallas kernels: 45.5 us -> 41.3 us  [back(): pl.pallas_call(functools.partial(back_body, ranks, shards), out_shape=(ja...]
    pallas_call x1, Pallas kernels: 65.5 us -> 62.4 us  [front(): pl.pallas_call(functools.partial(front_body, ranks, shards), out_shape=(j...]
    pallas_call x1, Pallas kernels: 25.5 us -> 22.9 us  [attend(): pl.pallas_call(functools.partial(attend_body, total, unroll), out_shape=(...]
    unnamed x18 -> x13, local copies, waits for them, and re-layouts: 7.51 us -> 6.03 us
  transfers between devices with their start and end apart: 1 -> 0, of which waited for: 0 -> 0; matrix products, arithmetic and copies ran while one was open for 0% -> 0% of each run, Pallas kernels for 57% -> 0%
where the time goes in v3:
time: 134 us; the launch traced here: 133 us
  Pallas kernels  127 us (95%)
  local copies, waits for them, and re-layouts  6.03 us (4%)
    pallas_call x1, Pallas kernels, front(): pl.pallas_call(functools.partial(front_body, ranks, shards), out_shape=(j...  62.4 us
    pallas_call x1, Pallas kernels, back(): pl.pallas_call(functools.partial(back_body, ranks, shards), out_shape=(ja...  41.3 us
    pallas_call x1, Pallas kernels, attend(): pl.pallas_call(functools.partial(attend_body, total, unroll), out_shape=(...  22.9 us
    unnamed x13, local copies, waits for them, and re-layouts  6.03 us

profile of v3, /device:TPU:1, one launch (start us, length us, event | category | flops | bytes accessed | tf_op | source)
XLA Modules:
  0.0 133.3 jit_solution(2324725935961823244)
XLA Ops:
  0.6 0.0 copy-start.4
  0.6 0.0 copy-start
  0.7 1.3 copy-done
  1.9 0.0 copy-start.2
  1.9 1.1 copy-done.2
  3.1 0.0 copy-start.3
  3.1 1.1 copy-done.3
  4.1 0.0 copy-start.1
  4.1 62.4 %front.1 = (bf16[3072,1536]{1,0:T(8,128)(2,1)S(1)}, bf16[3072,384]{1,0:T(8,128)(2,1)S(1)}, bf16[3072,128]{1,0:T(8,128)(2,1)S(1)}, bf16[4,2,4,4,96,384]{5,4,3,2,1,0:T(8,128)(2,1)S(1)}) custom-call(bf16[384,1536]{1,0:T(8,128)(2,1)S(1)} %bitcast.7, bf16[384,1024]{1,0:T(8,128)(2,1)S(1)} %bitcast.11, bf16[96,3072]{1,0:T(8,128)(2,1)S(1)} %copy-done.3), custom_call_target="tpu_custom_call" | custom-call | tf_op jit(solution)/shard_map/front/pallas_call | solution.py:308
  66.5 0.0 copy-done.4
  66.5 22.9 %attention.1 = (bf16[3072,128]{1,0:T(8,128)(2,1)S(1)}, bf16[3072,384]{1,0:T(8,128)(2,1)S(1)}) custom-call(s32[12]{0:T(128)S(1)} %bitcast.12, bf16[3072,384]{1,0:T(8,128)(2,1)S(1)} %get-tuple-element.12.qkv_ref, bf16[3072,128]{1,0:T(8,128)(2,1)S(1)} %get-tuple-element.13.do_ref), custom_call_target="tpu_custom_call" | custom-call | tf_op jit(solution)/shard_map/attention/pallas_call | solution.py:89
  89.4 0.0 copy-done.1
  89.4 41.3 %back.1 = (bf16[384,1024]{1,0:T(8,128)(2,1)S(1)}, bf16[384,1536]{1,0:T(8,128)(2,1)S(1)}, f32[96,384]{1,0:T(8,128)S(1)}) custom-call(bf16[3072,128]{1,0:T(8,128)(2,1)S(1)} %get-tuple-element.14.ctx, bf16[3072,384]{1,0:T(8,128)(2,1)S(1)} %get-tuple-element.15.grads, bf16[384,1536]{1,0:T(8,128)(2,1)S(1)} %bitcast.8, ...), custom_call_target="tpu_custom_call" | custom-call | tf_op jit(solution)/shard_map/back/pallas_call | solution.py:456
  130.7 0.9 copy.10
  131.6 1.0 copy.11
  132.6 0.7 copy.12
Async XLA Ops:
  0.6 65.9 %copy-start.4 = (s32[1,12]{1,0:T(1,128)S(1)}, s32[1,12]{1,0:T(1,128)}, u32[]{:S(2)}) copy-start(s32[1,12]{1,0:T(1,128)} %param.5) | copy-start | bytes 148
  0.6 1.3 copy-start
  1.9 1.1 copy-start.2
  3.1 1.1 copy-start.3
  4.1 85.3 %copy-start.1 = (bf16[1,384,1536]{2,1,0:T(8,128)(2,1)S(1)}, bf16[1,384,1536]{2,1,0:T(8,128)(2,1)}, u32[]{:S(2)}) copy-start(bf16[1,384,1536]{2,1,0:T(8,128)(2,1)} %param.4) | copy-start | bytes 3538948
